TPU v7x, 32 devices: a whole 2x2x4 slice. The times are simulated.
32 devices in a mesh: gz: 16 (over z, x, core), gy: 2 (over y).
Axes of the slice: x: 2, y: 2, z: 4, core: 2. Of those that a mesh axis runs over, the one named last changes fastest.
Arguments:
- spread_weights: float32 [64, 32768], P(None, ('gz', 'gy')), may hold values from -6 to 6
- spread_base: int32 [3, 32768], P(None, ('gz', 'gy')), may hold values from 0 to 383, as said below
- qm_base: int32 [3, 4096], P(None, ('gz', 'gy')), may hold values from 0 to 383, as said below
- qm_frac: float32 [3, 4096], P(None, ('gz', 'gy')), may hold values from 0 to 1
- qm_charge: float32 [4096], P(('gz', 'gy')), may hold values from -3 to 3
Outputs:
- qm_forces: float32 [3, 4096], P(None, ('gz', 'gy'))
Inputs may be any that keep to these rules, and one draw needn't show every extreme that they name: For point charge j let d = j // 1024, p = d // 2 and q = d % 2; then spread_base[0, j] lies in [p * 24, (p + 1) * 24) and spread_base[1, j] in [q * 192, (q + 1) * 192); spread_base[2, j] is any cell. For quantum-region atom i let d = i // 128, p = d // 2 and q = d % 2; then qm_base[0, i] lies in [p * 24, (p + 1) * 24) and qm_base[1, i] in [q * 192, (q + 1) * 192); qm_base[2, i] is any cell.
All inputs are finite; a program needn't handle non-finite values.
Results may differ from a plain program's by a relative error of at most 0.0003.
Values sent between devices are 32-bit elements; how exact they have to be, the bound alone decides.
A program may use at most 256 MiB of HBM per device.

v0:
```python
import math
import jax
import jax.numpy as jnp
from jax import lax
from jax.sharding import PartitionSpec as P

GRID = 384
ORDER = 4
SPLITTING = 0.8
HIGHEST = lax.Precision.HIGHEST


def passed_along(block, axis, distance):
    devices = range(lax.axis_size(axis))
    route = [((i - distance) % len(devices), i) for i in devices]
    return lax.ppermute(block, axis, route)


def moduli(index, points):
    signed = jnp.where(index < points // 2, index, index - points).astype(jnp.float32) / points
    spline = 2.0 / 3.0 + jnp.cos(2.0 * math.pi / points * index.astype(jnp.float32)) / 3.0
    return (signed * signed, 1.0 / (spline * spline), index == points // 2)


def influence(first, second, third, points):
    sq_one, mod_one, edge_one = moduli(first, points)
    sq_two, mod_two, edge_two = moduli(second, points)
    sq_three, mod_three, edge_three = moduli(third, points)
    total = sq_one + sq_two + sq_three
    safe = jnp.where(total > 0.0, total, 1.0)
    value = (
        mod_one
        * mod_two
        * mod_three
        * jnp.exp(-(math.pi * math.pi / (SPLITTING * SPLITTING)) * total)
        / (math.pi * safe)
    )
    keep = (total > 0.0) & jnp.logical_not(edge_one | edge_two | edge_three)
    return jnp.where(keep, value, 0.0)


def spline_weights(frac):
    remain = 1.0 - frac
    square = frac * frac
    cubed = square * frac
    values = jnp.stack(
        [
            remain * remain * remain / 6.0,
            (3.0 * cubed - 6.0 * square + 4.0) / 6.0,
            (-3.0 * cubed + 3.0 * square + 3.0 * frac + 1.0) / 6.0,
            cubed / 6.0,
        ]
    )
    slopes = jnp.stack(
        [
            -0.5 * remain * remain,
            (3.0 * square - 4.0 * frac) / 2.0,
            (-3.0 * square + 2.0 * frac + 1.0) / 2.0,
            0.5 * square,
        ]
    )
    return (values, slopes)


def angle_tables(rows_in, cols_in, points):
    product = rows_in[:, None] * cols_in[None, :] % points
    angle = 2.0 * math.pi / points * product.astype(jnp.float32)
    return (jnp.cos(angle), jnp.sin(angle))


def transform(real_part, imag_part, form, cosine, sine, sign):
    first = jnp.einsum(form, real_part, cosine, precision=HIGHEST)
    second = jnp.einsum(form, imag_part, sine, precision=HIGHEST)
    third = jnp.einsum(form, imag_part, cosine, precision=HIGHEST)
    fourth = jnp.einsum(form, real_part, sine, precision=HIGHEST)
    return (first - sign * second, third + sign * fourth)


def spread_grid(spread_weights, spread_base, z_first, y_first, z_extent, y_extent, points):
    count = spread_weights.shape[1]
    weights = spread_weights.reshape(ORDER, ORDER, ORDER, count)
    shifts = jnp.arange(ORDER, dtype=jnp.int32)
    local_z = spread_base[0] - z_first
    local_y = spread_base[1] - y_first
    plane_hits = (
        jnp.arange(z_extent, dtype=jnp.int32)[None, :, None]
        == local_z[None, None, :] + shifts[:, None, None]
    ).astype(jnp.float32)
    row_hits = (
        jnp.arange(y_extent, dtype=jnp.int32)[None, :, None]
        == local_y[None, None, :] + shifts[:, None, None]
    ).astype(jnp.float32)
    column_cells = (spread_base[2][None, :] + shifts[:, None]) % points
    column_hits = (
        jnp.arange(points, dtype=jnp.int32)[None, None, :] == column_cells[:, :, None]
    ).astype(jnp.float32)
    by_plane = jnp.sum(plane_hits[:, None, :, None, :] * weights[:, :, None, :, :], axis=0)
    placed = jnp.sum(by_plane[:, :, None, :, :] * row_hits[:, None, :, None, :], axis=0)
    charge = jnp.dot(
        placed.reshape(z_extent * y_extent, ORDER * count),
        column_hits.reshape(ORDER * count, points),
        precision=HIGHEST,
        preferred_element_type=jnp.float32,
    )
    return charge.reshape(z_extent, y_extent, points)


def line_tables(cells, values, slopes, extent):
    hits = (jnp.arange(extent, dtype=jnp.int32)[None, :, None] == cells[:, None, :]).astype(
        jnp.float32
    )
    return (jnp.sum(hits * values[:, None, :], axis=0), jnp.sum(hits * slopes[:, None, :], axis=0))


def interpolate(potential, qm_base, qm_frac, qm_charge, z_first, y_first):
    z_extent, y_extent, points = potential.shape
    count = qm_charge.shape[0]
    shifts = jnp.arange(ORDER, dtype=jnp.int32)[:, None]
    w_z, d_z = spline_weights(qm_frac[0])
    w_y, d_y = spline_weights(qm_frac[1])
    w_x, d_x = spline_weights(qm_frac[2])
    plane_w, plane_d = line_tables(qm_base[0][None, :] - z_first + shifts, w_z, d_z, z_extent)
    row_w, row_d = line_tables(qm_base[1][None, :] - y_first + shifts, w_y, d_y, y_extent)
    column_w, column_d = line_tables((qm_base[2][None, :] + shifts) % points, w_x, d_x, points)
    along_x = jnp.dot(
        potential.reshape(z_extent * y_extent, points),
        jnp.concatenate([column_w, column_d], axis=1),
        precision=HIGHEST,
        preferred_element_type=jnp.float32,
    ).reshape(z_extent, y_extent, 2, count)
    plain = along_x[:, :, 0, :]
    sloped = along_x[:, :, 1, :]
    force_z = jnp.sum(plain * plane_d[:, None, :] * row_w[None, :, :], axis=(0, 1))
    force_y = jnp.sum(plain * plane_w[:, None, :] * row_d[None, :, :], axis=(0, 1))
    force_x = jnp.sum(sloped * plane_w[:, None, :] * row_w[None, :, :], axis=(0, 1))
    return jnp.stack([-qm_charge * force_z, -qm_charge * force_y, -qm_charge * force_x])


def shards(spread_weights, spread_base, qm_base, qm_frac, qm_charge):
    points = GRID
    margin = ORDER - 1
    count_z = lax.axis_size("gz")
    count_y = lax.axis_size("gy")
    z_local = points // count_z
    y_local = points // count_y
    z_extent = z_local + margin
    y_extent = y_local + margin
    z_first = lax.axis_index("gz") * z_local
    y_first = lax.axis_index("gy") * y_local
    charge = spread_grid(spread_weights, spread_base, z_first, y_first, z_extent, y_extent, points)
    spill_rows = passed_along(charge[:, y_local:, :], "gy", 1)
    charge = charge[:, :y_local, :].at[:, :margin, :].add(spill_rows)
    spill_planes = passed_along(charge[z_local:], "gz", 1)
    charge = charge[:z_local].at[:margin].add(spill_planes)
    kx_count = points // 2
    kx_weight = jnp.where(jnp.arange(kx_count, dtype=jnp.int32) == 0, 1.0, 2.0).astype(jnp.float32)
    positions = jnp.arange(points, dtype=jnp.int32)
    cos_x, sin_x = angle_tables(positions, jnp.arange(kx_count, dtype=jnp.int32), points)
    real_x = jnp.einsum("zyx,xk->kyz", charge, cos_x, precision=HIGHEST)
    imag_x = -jnp.einsum("zyx,xk->kyz", charge, sin_x, precision=HIGHEST)
    packed = jnp.stack([real_x, imag_x]).reshape(2, kx_count, y_local * z_local)
    moved = lax.all_to_all(packed, "gy", split_axis=1, concat_axis=2, tiled=True)
    kx_local = kx_count // count_y
    lines = moved.reshape(2, kx_local, count_y, y_local, z_local)
    lines = lines.reshape(2, kx_local, points, z_local)
    cos_full, sin_full = angle_tables(positions, positions, points)
    real_y, imag_y = transform(lines[0], lines[1], "xyz,yk->kzx", cos_full, sin_full, -1.0)
    packed = jnp.stack([real_y, imag_y]).reshape(2, points, z_local * kx_local)
    moved = lax.all_to_all(packed, "gz", split_axis=1, concat_axis=2, tiled=True)
    ky_local = points // count_z
    lines = moved.reshape(2, ky_local, count_z, z_local, kx_local)
    lines = lines.reshape(2, ky_local, points, kx_local)
    real_z, imag_z = transform(lines[0], lines[1], "yzx,zk->yxk", cos_full, sin_full, -1.0)
    ky_index = lax.axis_index("gz") * ky_local + jnp.arange(ky_local, dtype=jnp.int32)
    kx_index = lax.axis_index("gy") * kx_local + jnp.arange(kx_local, dtype=jnp.int32)
    green = influence(
        positions[None, None, :], ky_index[:, None, None], kx_index[None, :, None], points
    )
    real_z = real_z * green
    imag_z = imag_z * green
    z_rows = (
        (
            jnp.arange(count_z, dtype=jnp.int32)[:, None] * z_local
            + jnp.arange(z_local, dtype=jnp.int32)[None, :]
        )
        % points
    ).reshape(-1)
    cos_z, sin_z = angle_tables(positions, z_rows, points)
    back_real, back_imag = transform(real_z, imag_z, "yxk,kp->pyx", cos_z, sin_z, 1.0)
    packed = jnp.stack([back_real, back_imag]).reshape(2, count_z * z_local, ky_local * kx_local)
    moved = lax.all_to_all(packed, "gz", split_axis=1, concat_axis=2, tiled=True).reshape(
        2, z_local, points, kx_local
    )
    y_rows = (
        (
            jnp.arange(count_y, dtype=jnp.int32)[:, None] * y_local
            + jnp.arange(y_local, dtype=jnp.int32)[None, :]
        )
        % points
    ).reshape(-1)
    cos_y, sin_y = angle_tables(positions, y_rows, points)
    back_real, back_imag = transform(moved[0], moved[1], "zkx,kp->pxz", cos_y, sin_y, 1.0)
    packed = jnp.stack([back_real, back_imag]).reshape(2, count_y * y_local, kx_local * z_local)
    moved = lax.all_to_all(packed, "gy", split_axis=1, concat_axis=2, tiled=True).reshape(
        2, y_local, kx_count, z_local
    )
    scale = 1.0 / float(points * points * points)
    potential = (
        jnp.einsum("ykz,xk->zyx", moved[0], cos_x * kx_weight[None, :], precision=HIGHEST)
        - jnp.einsum("ykz,xk->zyx", moved[1], sin_x * kx_weight[None, :], precision=HIGHEST)
    ) * scale
    rim_rows = passed_along(potential[:, :margin, :], "gy", -1)
    potential = jnp.concatenate([potential, rim_rows], axis=1)
    rim_planes = passed_along(potential[:margin], "gz", -1)
    potential = jnp.concatenate([potential, rim_planes], axis=0)
    return interpolate(potential, qm_base, qm_frac, qm_charge, z_first, y_first)


def solution(mesh):
    in_specs = (
        P(None, ("gz", "gy")),
        P(None, ("gz", "gy")),
        P(None, ("gz", "gy")),
        P(None, ("gz", "gy")),
        P(("gz", "gy")),
    )
    out_specs = P(None, ("gz", "gy"))
    return jax.shard_map(shards, mesh=mesh, in_specs=in_specs, out_specs=out_specs, check_vma=False)
```

profile of v0, /device:TPU:0, one launch (start us, length us, event | category | flops | bytes accessed | tf_op | source)
XLA Modules:
  0.0 1281.5 jit_solution(2450267871987228641)
XLA Ops:
  3.7 3.4 multiply_reduce_fusion.1
  7.1 158.1 %multiply_reduce_fusion = f32[27,195,4,1024]{3,2,1,0:T(4,128)} fusion(f32[4,195,1024]{2,1,0:T(8,128)S(1)} %fusion.18, f32[4,27,4,1024]{3,2,1,0:T(4,128)S(1)} %multiply_reduce_fusion.1), kind=kLoop, calls=%fused_computation | loop fusion | flops 150958080 | bytes 91226112 | tf_op jit(solution)/shard_map/reduce_sum | solution.py:98
  165.2 75.9 %dot_general.72 = f32[27,195,4096]{2,1,0:T(8,128)} reshape(f32[27,195,4,1024]{3,2,1,0:T(4,128)} %multiply_reduce_fusion) | data formatting | bytes 172523520 | tf_op jit(solution)/shard_map/dot_general | solution.py:99
  242.2 73.9 %fusion.6 = f32[27,195,384]{2,1,0:T(8,128)S(1)} fusion(f32[27,195,4096]{2,1,0:T(8,128)} %dot_general.72, pred[4096,384,1]{1,0,2:T(32,128)(4,1)S(1)} %fusion.280), kind=kOutput, calls=%fused_computation.18 | convolution fusion | flops 99373547520 | bytes 95921664 | tf_op jit(solution)/shard_map/dot_general | solution.py:99
  319.2 4.1 slice.163
  323.5 3.6 scatter-add.6
  328.4 3.7 slice.166
  332.1 11.5 collective-permute-done.1
  344.8 9.8 convolution_bitcast_fusion
  354.7 9.7 negate_bitcast_fusion
  369.8 4.2 pad_maximum_fusion
  374.1 11.4 copy.108
  385.5 80.2 %all_to_all.60 = f32[2,192,4608]{2,0,1:T(2,128)S(1)} all-to-all(f32[2,192,4608]{2,0,1:T(2,128)} %copy.108), channel_id=1, replica_groups=mesh['gz'=16,'gy'=2] {'gy'}, dimensions={1} | all-to-all | bytes 14155776 | tf_op jit(solution)/shard_map/all_to_all | solution.py:162
  469.4 3.4 copy.110
  472.9 3.8 copy.111
  476.6 10.3 fusion.44
  487.0 5.5 copy.112
  492.5 5.8 copy.113
  498.3 13.8 %fusion.42 = f32[384,96,24]{0,1,2:T(8,128)} fusion(f32[96,384,24]{1,0,2:T(8,128)} %copy.113), kind=kOutput, calls=%fused_computation.74 | convolution fusion | flops 4078190592 | bytes 7077888 | tf_op jit(solution)/shard_map/xyz,yk->kzx/dot_general | solution.py:74
  512.1 10.8 multiply_subtract_fusion
  522.9 8.9 copy.116
  531.8 14.2 %multiply_add_fusion = f32[384,96,24]{0,1,2:T(8,128)} fusion(f32[384,96,24]{0,1,2:T(8,128)} %fusion.42, f32[96,384,24]{1,0,2:T(8,128)S(1)} %copy.111), kind=kOutput, calls=%fused_computation.34 | convolution fusion | flops 4079960064 | bytes 10616832 | tf_op jit(solution)/shard_map/xyz,yk->kzx/dot_general | solution.py:75
  546.0 9.1 copy.117
  555.1 11.2 pad_maximum_fusion.1
  566.4 5.3 all-to-all-start.1
  574.6 124.7 %all-to-all-done.1 = f32[2,384,2304]{2,0,1:T(2,128)} async-done(((f32[2,384,2304]{2,0,1:T(2,128)}), f32[2,384,2304]{2,0,1:T(2,128)}, u32[]{:S(2)}, u32[]{:S(2)}) %all-to-all-start.1) | async-done | bytes 7077920 | tf_op jit(solution)/shard_map/all_to_all | solution.py:169
  699.4 3.6 copy.118
  706.3 6.2 squeeze.37
  712.5 15.8 %fusion.40 = f32[24,96,384]{2,1,0:T(8,128)} fusion(f32[24,384,96]{2,1,0:T(8,128)} %squeeze.37), kind=kOutput, calls=%fused_computation.72 | convolution fusion | flops 4078190592 | bytes 7077888 | tf_op jit(solution)/shard_map/yzx,zk->yxk/dot_general | solution.py:72
  731.1 6.4 squeeze.38
  737.6 15.0 %fusion.38 = f32[24,96,384]{2,1,0:T(8,128)S(1)} fusion(f32[24,384,96]{2,1,0:T(8,128)} %squeeze.38), kind=kOutput, calls=%fused_computation.70 | convolution fusion | flops 4078190592 | bytes 7077888 | tf_op jit(solution)/shard_map/yzx,zk->yxk/dot_general | solution.py:74
  752.6 14.8 %subtract_multiply_fusion = f32[24,96,384]{2,1,0:T(8,128)S(1)} fusion(f32[24,96,384]{2,1,0:T(8,128)S(1)} %copy-done.9, f32[24,384,96]{2,1,0:T(8,128)} %squeeze.38, f32[96]{0:T(128)S(1)} %copy-done.41, f32[24,384]{1,0:T(8,128)S(1)} %copy-done.11, pred[96]{0:T(512)(128)(4,1)S(1)} %copy-done.42, pred[24,384]{1,0:T(8,128)(4,1)S(1)} %broadcast_or_fusion, ...), kind=kOutput, calls=%fused_computation.33 | convolution fusion | flops 4091461632 | bytes 10700640 | tf_op jit(solution)/shard_map/yzx,zk->yxk/dot_general | solution.py:73
  767.5 12.5 add_multiply_fusion.1
  779.9 9.2 fusion.48
  789.2 10.7 fusion.46
  799.9 10.7 convolution_subtract_fusion
  810.6 8.9 copy.125
  819.5 13.8 %convolution_add_fusion = f32[384,24,96]{0,2,1:T(8,128)} fusion(f32[384,24,96]{0,2,1:T(8,128)} %fusion.46, f32[24,96,384]{2,1,0:T(8,128)S(1)} %subtract_multiply_fusion, s32[384]{0:T(512)S(1)} %add_select_fusion.7), kind=kOutput, calls=%fused_computation.47 | convolution fusion | flops 4079075328 | bytes 10618368 | tf_op jit(solution)/shard_map/yxk,kp->pyx/dot_general | solution.py:75
  833.3 9.3 copy.126
  842.6 11.2 pad_maximum_fusion.2
  853.9 31.3 %all-to-all-start.2 = ((f32[2,384,2304]{2,0,1:T(2,128)}), f32[2,384,2304]{2,0,1:T(2,128)}, u32[]{:S(2)}, u32[]{:S(2)}) async-start(f32[2,384,2304]{2,0,1:T(2,128)} %pad_maximum_fusion.2), calls=%async_computation.2 | async-start | bytes 14155776 | tf_op jit(solution)/shard_map/all_to_all | solution.py:191
  885.3 127.6 %all-to-all-done.2 = f32[2,384,2304]{2,0,1:T(2,128)} async-done(((f32[2,384,2304]{2,0,1:T(2,128)}), f32[2,384,2304]{2,0,1:T(2,128)}, u32[]{:S(2)}, u32[]{:S(2)}) %all-to-all-start.2) | async-done | bytes 7077920 | tf_op jit(solution)/shard_map/all_to_all | solution.py:191
  1012.9 3.6 copy.127
  1019.9 4.5 squeeze.40
  1024.4 4.2 copy.131
  1028.6 10.3 fusion.80
  1038.8 10.4 fusion.74
  1050.4 4.5 squeeze.39
  1054.9 4.0 copy.129
  1058.8 9.3 fusion.76
  1068.1 9.7 fusion.78
  1082.8 3.4 pad_maximum_fusion.3
  1086.2 12.3 copy.136
  1098.6 6.8 all-to-all-start.3
  1107.2 77.8 %all-to-all-done.3 = f32[2,384,2304]{2,0,1:T(2,128)} async-done(((f32[2,384,2304]{2,0,1:T(2,128)}), f32[2,384,2304]{2,0,1:T(2,128)}, u32[]{:S(2)}, u32[]{:S(2)}) %all-to-all-start.3) | async-done | bytes 7077920 | tf_op jit(solution)/shard_map/all_to_all | solution.py:204
  1185.0 3.6 copy.137
  1190.9 5.5 copy.140
  1196.4 3.6 copy.138
  1200.0 12.9 %fusion.8 = f32[384,192,24]{0,1,2:T(8,128)S(1)} fusion(f32[192,192,24]{0,2,1:T(8,128)} %bitcast.186, f32[192]{0:T(256)S(1)} %compare_select_fusion.3), kind=kOutput, calls=%fused_computation.19 | convolution fusion | flops 4077600768 | bytes 10617600 | tf_op jit(solution)/shard_map/ykz,xk->zyx/dot_general | solution.py:210
  1213.0 10.8 multiply_bitcast_fusion
  1224.2 5.6 collective-permute-done.2
  1229.9 27.0 %collective-permute-start.3 = (f32[3,195,384]{2,1,0:T(8,128)S(1)}, f32[3,195,384]{2,1,0:T(8,128)S(1)}, u32[]{:S(2)}, u32[]{:S(2)}) collective-permute-start(f32[3,195,384]{2,1,0:T(8,128)S(1)} %pad_maximum_fusion.4), channel_id=1, source_target_pairs={{2,0},{4,2},{6,4},{8,6},{10,8},{12,10},{14,12},{16,14},{18,16},{20... | collective-permute-start | bytes 2695688 | tf_op jit(solution)/shard_map/ppermute | solution.py:16
  1258.1 9.8 collective-permute-done.3
  1267.9 11.8 fusion
  (161 shorter events, 45.7 us)
Async XLA Ops:
  165.2 75.9 %copy-start.12 = (s32[1,1024]{1,0:T(1,128)S(1)}, s32[1,1024]{1,0:T(1,128)}, u32[]{:S(2)}) copy-start(s32[1,1024]{1,0:T(1,128)} %get-tuple-element.46) | copy-start | bytes 12292
  316.1 7.3 collective-permute-start
  328.3 15.2 %collective-permute-start.1 = (f32[3,192,384]{2,1,0:T(8,128)S(1)}, f32[3,192,384]{2,1,0:T(8,128)S(1)}, u32[]{:S(2)}, u32[]{:S(2)}) collective-permute-start(f32[3,192,384]{2,1,0:T(8,128)S(1)} %slice.168), channel_id=1, source_target_pairs={{30,0},{0,2},{2,4},{4,6},{6,8},{8,10},{10,12},{12,14},{14,16},{16,... | collective-permute-start | bytes 2654216 | tf_op jit(solution)/shard_map/ppermute | solution.py:16
  498.2 13.8 %copy-start.1 = (f32[96,384,24]{1,0,2:T(8,128)S(1)}, f32[96,384,24]{1,0,2:T(8,128)}, u32[]{:S(2)}) copy-start(f32[96,384,24]{1,0,2:T(8,128)} %copy.113) | copy-start | bytes 10616836
  498.2 13.8 %copy-start.2 = (f32[384,96,24]{0,1,2:T(8,128)S(1)}, f32[384,96,24]{0,1,2:T(8,128)}, u32[]{:S(2)}) copy-start(f32[384,96,24]{0,1,2:T(8,128)} %fusion.44) | copy-start | bytes 10616836
  546.0 9.1 copy-start.6
  566.4 133.0 %all-to-all-start.1 = ((f32[2,384,2304]{2,0,1:T(2,128)}), f32[2,384,2304]{2,0,1:T(2,128)}, u32[]{:S(2)}, u32[]{:S(2)}) async-start(f32[2,384,2304]{2,0,1:T(2,128)} %pad_maximum_fusion.1), calls=%async_computation.1 | async-start | bytes 14155776 | tf_op jit(solution)/shard_map/all_to_all | solution.py:169
  737.5 15.1 %copy-start.9 = (f32[24,96,384]{2,1,0:T(8,128)S(1)}, f32[24,96,384]{2,1,0:T(8,128)}, u32[]{:S(2)}) copy-start(f32[24,96,384]{2,1,0:T(8,128)} %fusion.40) | copy-start | bytes 10616836
  737.5 15.1 %copy-start.10 = (f32[24,384]{1,0:T(8,128)S(1)}, f32[24,384]{1,0:T(8,128)}, u32[]{:S(2)}) copy-start(f32[24,384]{1,0:T(8,128)} %broadcast_add_fusion) | copy-start | bytes 110596
  737.5 15.1 %copy-start.11 = (f32[24,384]{1,0:T(8,128)S(1)}, f32[24,384]{1,0:T(8,128)}, u32[]{:S(2)}) copy-start(f32[24,384]{1,0:T(8,128)} %broadcast_multiply_fusion) | copy-start | bytes 110596
  737.5 15.1 %copy-start.40 = (f32[96]{0:T(128)S(1)}, f32[96]{0:T(128)}, u32[]{:S(2)}) copy-start(f32[96]{0:T(128)} %get-tuple-element.81) | copy-start | bytes 1156
  737.5 15.1 %copy-start.41 = (f32[96]{0:T(128)S(1)}, f32[96]{0:T(128)}, u32[]{:S(2)}) copy-start(f32[96]{0:T(128)} %get-tuple-element.82) | copy-start | bytes 1156
  737.5 15.1 %copy-start.42 = (pred[96]{0:T(512)(128)(4,1)S(1)}, pred[96]{0:T(512)(128)(4,1)}, u32[]{:S(2)}) copy-start(pred[96]{0:T(512)(128)(4,1)} %fusion.189) | copy-start | bytes 292
  737.5 29.9 %slice-start = ((s8[4718592]{0:T(1024)(128)(4,1)}), s8[4194304]{0:T(1024)(128)(4,1)S(1)}, s32[]{:S(2)}) async-start(s8[4718592]{0:T(1024)(128)(4,1)} %bitcast.187), calls=%async_computation.4 | async-start | bytes 8388608
  752.6 14.8 %slice-start.1 = ((s8[4718592]{0:T(1024)(128)(4,1)}), s8[524288]{0:T(1024)(128)(4,1)S(1)}, s32[]{:S(2)}) async-start(s8[4718592]{0:T(1024)(128)(4,1)} %bitcast.187), calls=%async_computation.5 | async-start | bytes 1048576
  833.3 9.3 copy-start.5
  853.9 159.0 %all-to-all-start.2 = ((f32[2,384,2304]{2,0,1:T(2,128)}), f32[2,384,2304]{2,0,1:T(2,128)}, u32[]{:S(2)}, u32[]{:S(2)}) async-start(f32[2,384,2304]{2,0,1:T(2,128)} %pad_maximum_fusion.2), calls=%async_computation.2 | async-start | bytes 14155776 | tf_op jit(solution)/shard_map/all_to_all | solution.py:191
  1038.8 10.4 copy-start.4
  1068.1 9.7 copy-start.8
  1078.2 2.1 copy-start.7
  1098.6 6.8 copy-start.38
  1098.6 7.4 copy-start.13
  1098.6 86.5 %all-to-all-start.3 = ((f32[2,384,2304]{2,0,1:T(2,128)}), f32[2,384,2304]{2,0,1:T(2,128)}, u32[]{:S(2)}, u32[]{:S(2)}) async-start(f32[2,384,2304]{2,0,1:T(2,128)} %copy.136), calls=%async_computation.3 | async-start | bytes 14155776 | tf_op jit(solution)/shard_map/all_to_all | solution.py:204
  1200.0 12.9 %copy-start.3 = (f32[1,192,2,2304]{1,3,2,0:T(8,128)S(1)}, f32[1,192,2,2304]{1,3,2,0:T(8,128)}, u32[]{:S(2)}) copy-start(f32[1,192,2,2304]{1,3,2,0:T(8,128)} %copy.138) | copy-start | bytes 10616836
  1212.9 11.0 copy-start.29
  1213.0 11.0 copy-start.30
  1213.0 11.0 copy-start.31
  1213.0 11.0 copy-start.32
  1213.0 11.0 copy-start.33
  1213.0 11.0 copy-start.34
  1213.0 11.0 copy-start.35
  1213.0 11.0 copy-start.36
  1223.8 6.0 copy-start
  1223.9 5.9 collective-permute-start.2
  1224.1 33.2 %copy-start.16 = (f32[1,128]{1,0:T(1,128)S(1)}, f32[1,128]{1,0:T(1,128)}, u32[]{:S(2)}) copy-start(f32[1,128]{1,0:T(1,128)} %get-tuple-element.71) | copy-start | bytes 1540
  1224.1 33.2 %copy-start.22 = (f32[1,128]{1,0:T(1,128)S(1)}, f32[1,128]{1,0:T(1,128)}, u32[]{:S(2)}) copy-start(f32[1,128]{1,0:T(1,128)} %get-tuple-element.57) | copy-start | bytes 1540
  1224.1 33.2 %copy-start.23 = (f32[1,128]{1,0:T(1,128)S(1)}, f32[1,128]{1,0:T(1,128)}, u32[]{:S(2)}) copy-start(f32[1,128]{1,0:T(1,128)} %get-tuple-element.58) | copy-start | bytes 1540
  1224.1 33.2 %copy-start.24 = (f32[1,128]{1,0:T(1,128)S(1)}, f32[1,128]{1,0:T(1,128)}, u32[]{:S(2)}) copy-start(f32[1,128]{1,0:T(1,128)} %get-tuple-element.59) | copy-start | bytes 1540
  1224.1 33.2 %copy-start.25 = (f32[1,128]{1,0:T(1,128)S(1)}, f32[1,128]{1,0:T(1,128)}, u32[]{:S(2)}) copy-start(f32[1,128]{1,0:T(1,128)} %get-tuple-element.63) | copy-start | bytes 1540
  1224.1 33.2 %copy-start.26 = (f32[1,128]{1,0:T(1,128)S(1)}, f32[1,128]{1,0:T(1,128)}, u32[]{:S(2)}) copy-start(f32[1,128]{1,0:T(1,128)} %get-tuple-element.64) | copy-start | bytes 1540
  1224.1 33.2 %copy-start.27 = (f32[1,128]{1,0:T(1,128)S(1)}, f32[1,128]{1,0:T(1,128)}, u32[]{:S(2)}) copy-start(f32[1,128]{1,0:T(1,128)} %get-tuple-element.65) | copy-start | bytes 1540
  1224.1 33.2 %copy-start.28 = (f32[1,128]{1,0:T(1,128)S(1)}, f32[1,128]{1,0:T(1,128)}, u32[]{:S(2)}) copy-start(f32[1,128]{1,0:T(1,128)} %get-tuple-element.66) | copy-start | bytes 1540
  1224.1 33.2 %copy-start.14 = (f32[1,128]{1,0:T(1,128)S(1)}, f32[1,128]{1,0:T(1,128)}, u32[]{:S(2)}) copy-start(f32[1,128]{1,0:T(1,128)} %get-tuple-element.73) | copy-start | bytes 1540
  1224.1 33.2 %copy-start.15 = (f32[1,128]{1,0:T(1,128)S(1)}, f32[1,128]{1,0:T(1,128)}, u32[]{:S(2)}) copy-start(f32[1,128]{1,0:T(1,128)} %get-tuple-element.75) | copy-start | bytes 1540
  1224.2 33.2 %copy-start.17 = (f32[1,128]{1,0:T(1,128)S(1)}, f32[1,128]{1,0:T(1,128)}, u32[]{:S(2)}) copy-start(f32[1,128]{1,0:T(1,128)} %get-tuple-element.49) | copy-start | bytes 1540
  1224.2 33.2 %copy-start.18 = (f32[1,128]{1,0:T(1,128)S(1)}, f32[1,128]{1,0:T(1,128)}, u32[]{:S(2)}) copy-start(f32[1,128]{1,0:T(1,128)} %get-tuple-element.60) | copy-start | bytes 1540
  1224.2 33.2 %copy-start.19 = (f32[1,128]{1,0:T(1,128)S(1)}, f32[1,128]{1,0:T(1,128)}, u32[]{:S(2)}) copy-start(f32[1,128]{1,0:T(1,128)} %get-tuple-element.61) | copy-start | bytes 1540
  1224.2 33.2 %copy-start.20 = (f32[1,128]{1,0:T(1,128)S(1)}, f32[1,128]{1,0:T(1,128)}, u32[]{:S(2)}) copy-start(f32[1,128]{1,0:T(1,128)} %get-tuple-element.62) | copy-start | bytes 1540
  1224.2 33.2 %copy-start.21 = (f32[1,128]{1,0:T(1,128)S(1)}, f32[1,128]{1,0:T(1,128)}, u32[]{:S(2)}) copy-start(f32[1,128]{1,0:T(1,128)} %get-tuple-element.67) | copy-start | bytes 1540
  1224.2 33.3 %copy-start.37 = (s32[128]{0:T(128)S(1)}, s32[128]{0:T(128)}, u32[]{:S(2)}) copy-start(s32[128]{0:T(128)} %get-tuple-element.68) | copy-start | bytes 1540
  1229.9 38.0 %collective-permute-start.3 = (f32[3,195,384]{2,1,0:T(8,128)S(1)}, f32[3,195,384]{2,1,0:T(8,128)S(1)}, u32[]{:S(2)}, u32[]{:S(2)}) collective-permute-start(f32[3,195,384]{2,1,0:T(8,128)S(1)} %pad_maximum_fusion.4), channel_id=1, source_target_pairs={{2,0},{4,2},{6,4},{8,6},{10,8},{12,10},{14,12},{16,14},{18,16},{20... | collective-permute-start | bytes 2695688 | tf_op jit(solution)/shard_map/ppermute | solution.py:16
  1279.7 0.9 copy-start.39
where the time goes:
time: 1290 us; the launch traced here: 1280 us
  waiting for transfers between devices  357 us (28%)
  matrix products  320 us (25%)
  local copies, waits for them, and re-layouts  245 us (19%)
  other arithmetic  205 us (16%)
  blocking collectives  80.2 us (6%)
  starting transfers between devices  73.5 us (6%)
    all_to_all x2, waiting for transfers between devices, shards(): lax.all_to_all(packed, 'gz', split_axis=1, concat_axis=2, tiled=True)  252 us
    reduce_sum x1, other arithmetic, spread_grid(): jnp.sum(by_plane[:, :, None, :, :] * row_hits[:, None, :, None, :], axis=0)  158 us
    all_to_all x1, blocking collectives, shards(): lax.all_to_all(packed, 'gy', split_axis=1, concat_axis=2, tiled=True)  80.2 us
    all_to_all x1, waiting for transfers between devices, shards(): lax.all_to_all(packed, 'gy', split_axis=1, concat_axis=2, tiled=True)  77.8 us
    dot_general x1, local copies, waits for them, and re-layouts, spread_grid(): jnp.dot(placed.reshape(z_extent * y_extent, ORDER * count), column_hits.r...  75.9 us
    dot_general x1, matrix products, spread_grid(): jnp.dot(placed.reshape(z_extent * y_extent, ORDER * count), column_hits.r...  73.9 us
    dot_general x3, matrix products, transform(): fourth = jnp.einsum(form, real_part, sine, precision=HIGHEST)  40.4 us
    unnamed x4, matrix products  39.6 us
  transfers between devices with their start and end apart: 7, of which 7 were waited for; matrix products, arithmetic and copies ran while one was open for 1% of the time, Pallas kernels for 0%

commit v1 on v0

--- a/solution.py
+++ b/solution.py
@@ -8,6 +8,13 @@
 ORDER = 4
 SPLITTING = 0.8
 HIGHEST = lax.Precision.HIGHEST
+
+
+def _step_on_bars(frame, link_axis):
+    main = lax.axis_size(link_axis)
+    before = jnp.stack(jnp.split(frame, main, 1), 0)
+    aux = jnp.concatenate(lax.all_to_all(before, link_axis, split_axis=0, concat_axis=0), 2)
+    return aux
 
 
 def passed_along(block, axis, distance):
@@ -166,7 +173,7 @@
     cos_full, sin_full = angle_tables(positions, positions, points)
     real_y, imag_y = transform(lines[0], lines[1], "xyz,yk->kzx", cos_full, sin_full, -1.0)
     packed = jnp.stack([real_y, imag_y]).reshape(2, points, z_local * kx_local)
-    moved = lax.all_to_all(packed, "gz", split_axis=1, concat_axis=2, tiled=True)
+    moved = _step_on_bars(packed, "gz")
     ky_local = points // count_z
     lines = moved.reshape(2, ky_local, count_z, z_local, kx_local)
     lines = lines.reshape(2, ky_local, points, kx_local)

time: 1290 us -> 1280 us (level)
    all_to_all x0 -> x1, waiting for transfers between devices: none -> 125 us  [_step_on_bars(): lax.all_to_all(before, link_axis, split_axis=0, concat_axis=0)]
    all_to_all x2 -> x1, waiting for transfers between devices: 252 us -> 128 us  [shards(): lax.all_to_all(packed, 'gz', split_axis=1, concat_axis=2, tiled=True)]
    unnamed x1 -> x16, other arithmetic: 0.01 us -> 13.3 us
    all_to_all x2 -> x1, starting transfers between devices: 36.5 us -> 31.3 us  [shards(): lax.all_to_all(packed, 'gz', split_axis=1, concat_axis=2, tiled=True)]
where the time goes in v1:
time: 1280 us; the launch traced here: 1270 us
  waiting for transfers between devices  357 us (28%)
  matrix products  317 us (25%)
  local copies, waits for them, and re-layouts  233 us (18%)
  other arithmetic  208 us (16%)
  blocking collectives  80.2 us (6%)
  starting transfers between devices  73.3 us (6%)
    reduce_sum x1, other arithmetic, spread_grid(): jnp.sum(by_plane[:, :, None, :, :] * row_hits[:, None, :, None, :], axis=0)  158 us
    all_to_all x1, waiting for transfers between devices, shards(): lax.all_to_all(packed, 'gz', split_axis=1, concat_axis=2, tiled=True)  128 us
    all_to_all x1, waiting for transfers between devices, _step_on_bars(): lax.all_to_all(before, link_axis, split_axis=0, concat_axis=0)  125 us
    all_to_all x1, blocking collectives, shards(): lax.all_to_all(packed, 'gy', split_axis=1, concat_axis=2, tiled=True)  80.2 us
    all_to_all x1, waiting for transfers between devices, shards(): lax.all_to_all(packed, 'gy', split_axis=1, concat_axis=2, tiled=True)  77.8 us
    dot_general x1, local copies, waits for them, and re-layouts, spread_grid(): jnp.dot(placed.reshape(z_extent * y_extent, ORDER * count), column_hits.r...  75.9 us
    dot_general x1, matrix products, spread_grid(): jnp.dot(placed.reshape(z_extent * y_extent, ORDER * count), column_hits.r...  73.9 us
    dot_general x3, matrix products, transform(): fourth = jnp.einsum(form, real_part, sine, precision=HIGHEST)  40.5 us
  transfers between devices with their start and end apart: 7, of which 7 were waited for; matrix products, arithmetic and copies ran while one was open for 1% of the time, Pallas kernels for 0%

profile of v1, /device:TPU:0, one launch (start us, length us, event | category | flops | bytes accessed | tf_op | source)
XLA Modules:
  0.0 1269.4 jit_solution(15730643072253990759)
XLA Ops:
  3.7 3.4 multiply_reduce_fusion.1
  7.1 158.1 %multiply_reduce_fusion = f32[27,195,4,1024]{3,2,1,0:T(4,128)} fusion(f32[4,195,1024]{2,1,0:T(8,128)S(1)} %fusion.18, f32[4,27,4,1024]{3,2,1,0:T(4,128)S(1)} %multiply_reduce_fusion.1), kind=kLoop, calls=%fused_computation | loop fusion | flops 150958080 | bytes 91226112 | tf_op jit(solution)/shard_map/reduce_sum | solution.py:105
  165.2 75.9 %dot_general.72 = f32[27,195,4096]{2,1,0:T(8,128)} reshape(f32[27,195,4,1024]{3,2,1,0:T(4,128)} %multiply_reduce_fusion) | data formatting | bytes 172523520 | tf_op jit(solution)/shard_map/dot_general | solution.py:106
  242.2 73.9 %fusion.6 = f32[27,195,384]{2,1,0:T(8,128)S(1)} fusion(f32[27,195,4096]{2,1,0:T(8,128)} %dot_general.72, pred[4096,384,1]{1,0,2:T(32,128)(4,1)S(1)} %fusion.297), kind=kOutput, calls=%fused_computation.47 | convolution fusion | flops 99373547520 | bytes 95921664 | tf_op jit(solution)/shard_map/dot_general | solution.py:106
  316.1 3.1 collective-permute-start
  319.2 4.1 slice.163
  323.5 3.6 scatter-add.6
  328.4 3.7 slice.166
  332.1 11.5 collective-permute-done.1
  344.8 9.8 convolution_bitcast_fusion
  354.7 9.7 negate_bitcast_fusion
  369.8 4.2 pad_maximum_fusion
  374.1 11.4 copy.133
  385.5 80.2 %all_to_all.50 = f32[2,192,4608]{2,0,1:T(2,128)S(1)} all-to-all(f32[2,192,4608]{2,0,1:T(2,128)} %copy.133), channel_id=1, replica_groups=mesh['gz'=16,'gy'=2] {'gy'}, dimensions={1} | all-to-all | bytes 14155776 | tf_op jit(solution)/shard_map/all_to_all | solution.py:169
  469.4 3.4 copy.135
  472.9 3.8 copy.136
  476.7 10.3 fusion.44
  486.9 5.5 copy.137
  492.5 3.9 copy.138
  496.4 10.2 fusion.42
  506.7 10.9 multiply_subtract_fusion
  517.6 3.3 copy.141
  520.9 14.3 %multiply_add_fusion = f32[384,96,24]{0,1,2:T(8,128)} fusion(f32[384,96,24]{0,1,2:T(8,128)} %fusion.42, f32[96,384,24]{1,0,2:T(8,128)} %copy-done.2), kind=kOutput, calls=%fused_computation.63 | convolution fusion | flops 4079960064 | bytes 10616832 | tf_op jit(solution)/shard_map/xyz,yk->kzx/dot_general | solution.py:82
  535.2 5.3 copy.142
  554.9 5.1 all-to-all-start.1
  563.0 124.8 %all-to-all-done.1 = f32[16,2,24,2304]{3,2,1,0:T(8,128)} async-done(((f32[16,2,24,2304]{3,2,1,0:T(8,128)}), f32[16,2,24,2304]{3,2,1,0:T(8,128)}, u32[]{:S(2)}, u32[]{:S(2)}) %all-to-all-start.1) | async-done | bytes 7077920 | tf_op jit(solution)/shard_map/all_to_all | solution.py:16
  687.8 3.5 fusion.271
  694.2 6.2 squeeze.37
  700.4 15.8 %fusion.40 = f32[24,96,384]{2,1,0:T(8,128)} fusion(f32[24,384,96]{2,1,0:T(8,128)} %squeeze.37), kind=kOutput, calls=%fused_computation.101 | convolution fusion | flops 4078190592 | bytes 7077888 | tf_op jit(solution)/shard_map/yzx,zk->yxk/dot_general | solution.py:79
  719.0 6.4 squeeze.38
  725.4 15.0 %fusion.38 = f32[24,96,384]{2,1,0:T(8,128)S(1)} fusion(f32[24,384,96]{2,1,0:T(8,128)} %squeeze.38), kind=kOutput, calls=%fused_computation.99 | convolution fusion | flops 4078190592 | bytes 7077888 | tf_op jit(solution)/shard_map/yzx,zk->yxk/dot_general | solution.py:81
  740.5 14.8 %subtract_multiply_fusion = f32[24,96,384]{2,1,0:T(8,128)S(1)} fusion(f32[24,96,384]{2,1,0:T(8,128)S(1)} %copy-done.9, f32[24,384,96]{2,1,0:T(8,128)} %squeeze.38, f32[96]{0:T(128)S(1)} %copy-done.41, f32[24,384]{1,0:T(8,128)S(1)} %copy-done.11, pred[96]{0:T(512)(128)(4,1)S(1)} %copy-done.42, pred[24,384]{1,0:T(8,128)(4,1)S(1)} %broadcast_or_fusion, ...), kind=kOutput, calls=%fused_computation.62 | convolution fusion | flops 4091461632 | bytes 10700640 | tf_op jit(solution)/shard_map/yzx,zk->yxk/dot_general | solution.py:80
  755.4 12.5 add_multiply_fusion.1
  767.8 9.2 fusion.48
  777.1 10.7 fusion.46
  787.7 10.7 convolution_subtract_fusion
  798.5 8.9 copy.149
  807.4 13.8 %convolution_add_fusion = f32[384,24,96]{0,2,1:T(8,128)} fusion(f32[384,24,96]{0,2,1:T(8,128)} %fusion.46, f32[24,96,384]{2,1,0:T(8,128)S(1)} %subtract_multiply_fusion, s32[384]{0:T(512)S(1)} %add_select_fusion.7), kind=kOutput, calls=%fused_computation.76 | convolution fusion | flops 4079075328 | bytes 10618368 | tf_op jit(solution)/shard_map/yxk,kp->pyx/dot_general | solution.py:82
  821.2 9.3 copy.150
  830.5 11.2 pad_maximum_fusion.1
  841.8 31.3 %all-to-all-start.2 = ((f32[2,384,2304]{2,0,1:T(2,128)}), f32[2,384,2304]{2,0,1:T(2,128)}, u32[]{:S(2)}, u32[]{:S(2)}) async-start(f32[2,384,2304]{2,0,1:T(2,128)} %pad_maximum_fusion.1), calls=%async_computation.2 | async-start | bytes 14155776 | tf_op jit(solution)/shard_map/all_to_all | solution.py:198
  873.2 127.6 %all-to-all-done.2 = f32[2,384,2304]{2,0,1:T(2,128)} async-done(((f32[2,384,2304]{2,0,1:T(2,128)}), f32[2,384,2304]{2,0,1:T(2,128)}, u32[]{:S(2)}, u32[]{:S(2)}) %all-to-all-start.2) | async-done | bytes 7077920 | tf_op jit(solution)/shard_map/all_to_all | solution.py:198
  1000.8 3.6 copy.151
  1007.8 4.5 squeeze.40
  1012.3 4.2 copy.155
  1016.5 10.3 fusion.80
  1026.7 10.4 fusion.74
  1038.2 4.5 squeeze.39
  1042.7 4.0 copy.153
  1046.7 9.3 fusion.76
  1056.0 9.7 fusion.78
  1070.7 3.4 pad_maximum_fusion.2
  1074.1 12.3 copy.160
  1086.4 6.8 all-to-all-start.3
  1095.1 77.8 %all-to-all-done.3 = f32[2,384,2304]{2,0,1:T(2,128)} async-done(((f32[2,384,2304]{2,0,1:T(2,128)}), f32[2,384,2304]{2,0,1:T(2,128)}, u32[]{:S(2)}, u32[]{:S(2)}) %all-to-all-start.3) | async-done | bytes 7077920 | tf_op jit(solution)/shard_map/all_to_all | solution.py:211
  1172.9 3.6 copy.161
  1178.8 5.5 copy.164
  1184.3 3.6 copy.162
  1187.9 12.9 %fusion.8 = f32[384,192,24]{0,1,2:T(8,128)S(1)} fusion(f32[192,192,24]{0,2,1:T(8,128)} %bitcast.217, f32[192]{0:T(256)S(1)} %compare_select_fusion.3), kind=kOutput, calls=%fused_computation.48 | convolution fusion | flops 4077600768 | bytes 10617600 | tf_op jit(solution)/shard_map/ykz,xk->zyx/dot_general | solution.py:217
  1200.9 10.8 multiply_bitcast_fusion
  1212.1 5.6 collective-permute-done.2
  1217.8 27.0 %collective-permute-start.3 = (f32[3,195,384]{2,1,0:T(8,128)S(1)}, f32[3,195,384]{2,1,0:T(8,128)S(1)}, u32[]{:S(2)}, u32[]{:S(2)}) collective-permute-start(f32[3,195,384]{2,1,0:T(8,128)S(1)} %pad_maximum_fusion.3), channel_id=1, source_target_pairs={{2,0},{4,2},{6,4},{8,6},{10,8},{12,10},{14,12},{16,14},{18,16},{20... | collective-permute-start | bytes 2695688 | tf_op jit(solution)/shard_map/ppermute | solution.py:23
  1245.9 9.8 collective-permute-done.3
  1255.8 11.8 fusion
  (175 shorter events, 56.5 us)
Async XLA Ops:
  165.2 75.9 %copy-start.12 = (s32[1,1024]{1,0:T(1,128)S(1)}, s32[1,1024]{1,0:T(1,128)}, u32[]{:S(2)}) copy-start(s32[1,1024]{1,0:T(1,128)} %get-tuple-element.46) | copy-start | bytes 12292
  316.1 7.3 collective-permute-start
  328.3 15.2 %collective-permute-start.1 = (f32[3,192,384]{2,1,0:T(8,128)S(1)}, f32[3,192,384]{2,1,0:T(8,128)S(1)}, u32[]{:S(2)}, u32[]{:S(2)}) collective-permute-start(f32[3,192,384]{2,1,0:T(8,128)S(1)} %slice.168), channel_id=1, source_target_pairs={{30,0},{0,2},{2,4},{4,6},{6,8},{8,10},{10,12},{12,14},{14,16},{16,... | collective-permute-start | bytes 2654216 | tf_op jit(solution)/shard_map/ppermute | solution.py:23
  476.6 10.3 copy-start.2
  496.4 10.2 copy-start.3
  540.5 2.2 copy-start
  554.9 132.8 %all-to-all-start.1 = ((f32[16,2,24,2304]{3,2,1,0:T(8,128)}), f32[16,2,24,2304]{3,2,1,0:T(8,128)}, u32[]{:S(2)}, u32[]{:S(2)}) async-start(f32[16,2,24,2304]{3,2,1,0:T(8,128)} %fusion.102), calls=%async_computation.1 | async-start | bytes 14155776 | tf_op jit(solution)/shard_map/all_to_all | solution.py:16
  725.4 15.1 %copy-start.9 = (f32[24,96,384]{2,1,0:T(8,128)S(1)}, f32[24,96,384]{2,1,0:T(8,128)}, u32[]{:S(2)}) copy-start(f32[24,96,384]{2,1,0:T(8,128)} %fusion.40) | copy-start | bytes 10616836
  725.4 15.1 %copy-start.10 = (f32[24,384]{1,0:T(8,128)S(1)}, f32[24,384]{1,0:T(8,128)}, u32[]{:S(2)}) copy-start(f32[24,384]{1,0:T(8,128)} %broadcast_add_fusion) | copy-start | bytes 110596
  725.4 15.1 %copy-start.11 = (f32[24,384]{1,0:T(8,128)S(1)}, f32[24,384]{1,0:T(8,128)}, u32[]{:S(2)}) copy-start(f32[24,384]{1,0:T(8,128)} %broadcast_multiply_fusion) | copy-start | bytes 110596
  725.4 15.1 %copy-start.40 = (f32[96]{0:T(128)S(1)}, f32[96]{0:T(128)}, u32[]{:S(2)}) copy-start(f32[96]{0:T(128)} %get-tuple-element.81) | copy-start | bytes 1156
  725.4 15.1 %copy-start.41 = (f32[96]{0:T(128)S(1)}, f32[96]{0:T(128)}, u32[]{:S(2)}) copy-start(f32[96]{0:T(128)} %get-tuple-element.82) | copy-start | bytes 1156
  725.4 15.1 %copy-start.42 = (pred[96]{0:T(512)(128)(4,1)S(1)}, pred[96]{0:T(512)(128)(4,1)}, u32[]{:S(2)}) copy-start(pred[96]{0:T(512)(128)(4,1)} %fusion.206) | copy-start | bytes 292
  725.4 29.9 %slice-start = ((s8[4718592]{0:T(1024)(128)(4,1)}), s8[4194304]{0:T(1024)(128)(4,1)S(1)}, s32[]{:S(2)}) async-start(s8[4718592]{0:T(1024)(128)(4,1)} %bitcast.218), calls=%async_computation.4 | async-start | bytes 8388608
  740.5 14.8 %slice-start.1 = ((s8[4718592]{0:T(1024)(128)(4,1)}), s8[524288]{0:T(1024)(128)(4,1)S(1)}, s32[]{:S(2)}) async-start(s8[4718592]{0:T(1024)(128)(4,1)} %bitcast.218), calls=%async_computation.5 | async-start | bytes 1048576
  821.2 9.3 copy-start.6
  841.8 159.0 %all-to-all-start.2 = ((f32[2,384,2304]{2,0,1:T(2,128)}), f32[2,384,2304]{2,0,1:T(2,128)}, u32[]{:S(2)}, u32[]{:S(2)}) async-start(f32[2,384,2304]{2,0,1:T(2,128)} %pad_maximum_fusion.1), calls=%async_computation.2 | async-start | bytes 14155776 | tf_op jit(solution)/shard_map/all_to_all | solution.py:198
  1026.7 10.4 copy-start.5
  1056.0 9.7 copy-start.8
  1066.1 2.1 copy-start.7
  1086.4 6.8 copy-start.38
  1086.4 7.4 copy-start.13
  1086.4 86.5 %all-to-all-start.3 = ((f32[2,384,2304]{2,0,1:T(2,128)}), f32[2,384,2304]{2,0,1:T(2,128)}, u32[]{:S(2)}, u32[]{:S(2)}) async-start(f32[2,384,2304]{2,0,1:T(2,128)} %copy.160), calls=%async_computation.3 | async-start | bytes 14155776 | tf_op jit(solution)/shard_map/all_to_all | solution.py:211
  1187.9 12.9 %copy-start.4 = (f32[1,192,2,2304]{1,3,2,0:T(8,128)S(1)}, f32[1,192,2,2304]{1,3,2,0:T(8,128)}, u32[]{:S(2)}) copy-start(f32[1,192,2,2304]{1,3,2,0:T(8,128)} %copy.162) | copy-start | bytes 10616836
  1200.8 11.0 copy-start.29
  1200.8 11.0 copy-start.30
  1200.9 11.0 copy-start.31
  1200.9 11.0 copy-start.32
  1200.9 11.0 copy-start.33
  1200.9 11.0 copy-start.34
  1200.9 11.0 copy-start.35
  1200.9 11.0 copy-start.36
  1211.7 6.0 copy-start.1
  1211.8 5.9 collective-permute-start.2
  1211.9 33.2 %copy-start.16 = (f32[1,128]{1,0:T(1,128)S(1)}, f32[1,128]{1,0:T(1,128)}, u32[]{:S(2)}) copy-start(f32[1,128]{1,0:T(1,128)} %get-tuple-element.71) | copy-start | bytes 1540
  1212.0 33.2 %copy-start.22 = (f32[1,128]{1,0:T(1,128)S(1)}, f32[1,128]{1,0:T(1,128)}, u32[]{:S(2)}) copy-start(f32[1,128]{1,0:T(1,128)} %get-tuple-element.57) | copy-start | bytes 1540
  1212.0 33.2 %copy-start.23 = (f32[1,128]{1,0:T(1,128)S(1)}, f32[1,128]{1,0:T(1,128)}, u32[]{:S(2)}) copy-start(f32[1,128]{1,0:T(1,128)} %get-tuple-element.58) | copy-start | bytes 1540
  1212.0 33.2 %copy-start.24 = (f32[1,128]{1,0:T(1,128)S(1)}, f32[1,128]{1,0:T(1,128)}, u32[]{:S(2)}) copy-start(f32[1,128]{1,0:T(1,128)} %get-tuple-element.59) | copy-start | bytes 1540
  1212.0 33.2 %copy-start.25 = (f32[1,128]{1,0:T(1,128)S(1)}, f32[1,128]{1,0:T(1,128)}, u32[]{:S(2)}) copy-start(f32[1,128]{1,0:T(1,128)} %get-tuple-element.63) | copy-start | bytes 1540
  1212.0 33.2 %copy-start.26 = (f32[1,128]{1,0:T(1,128)S(1)}, f32[1,128]{1,0:T(1,128)}, u32[]{:S(2)}) copy-start(f32[1,128]{1,0:T(1,128)} %get-tuple-element.64) | copy-start | bytes 1540
  1212.0 33.2 %copy-start.27 = (f32[1,128]{1,0:T(1,128)S(1)}, f32[1,128]{1,0:T(1,128)}, u32[]{:S(2)}) copy-start(f32[1,128]{1,0:T(1,128)} %get-tuple-element.65) | copy-start | bytes 1540
  1212.0 33.2 %copy-start.28 = (f32[1,128]{1,0:T(1,128)S(1)}, f32[1,128]{1,0:T(1,128)}, u32[]{:S(2)}) copy-start(f32[1,128]{1,0:T(1,128)} %get-tuple-element.66) | copy-start | bytes 1540
  1212.0 33.2 %copy-start.14 = (f32[1,128]{1,0:T(1,128)S(1)}, f32[1,128]{1,0:T(1,128)}, u32[]{:S(2)}) copy-start(f32[1,128]{1,0:T(1,128)} %get-tuple-element.73) | copy-start | bytes 1540
  1212.0 33.2 %copy-start.15 = (f32[1,128]{1,0:T(1,128)S(1)}, f32[1,128]{1,0:T(1,128)}, u32[]{:S(2)}) copy-start(f32[1,128]{1,0:T(1,128)} %get-tuple-element.75) | copy-start | bytes 1540
  1212.0 33.2 %copy-start.17 = (f32[1,128]{1,0:T(1,128)S(1)}, f32[1,128]{1,0:T(1,128)}, u32[]{:S(2)}) copy-start(f32[1,128]{1,0:T(1,128)} %get-tuple-element.49) | copy-start | bytes 1540
  1212.1 33.2 %copy-start.18 = (f32[1,128]{1,0:T(1,128)S(1)}, f32[1,128]{1,0:T(1,128)}, u32[]{:S(2)}) copy-start(f32[1,128]{1,0:T(1,128)} %get-tuple-element.60) | copy-start | bytes 1540
  1212.1 33.2 %copy-start.19 = (f32[1,128]{1,0:T(1,128)S(1)}, f32[1,128]{1,0:T(1,128)}, u32[]{:S(2)}) copy-start(f32[1,128]{1,0:T(1,128)} %get-tuple-element.61) | copy-start | bytes 1540
  1212.1 33.2 %copy-start.20 = (f32[1,128]{1,0:T(1,128)S(1)}, f32[1,128]{1,0:T(1,128)}, u32[]{:S(2)}) copy-start(f32[1,128]{1,0:T(1,128)} %get-tuple-element.62) | copy-start | bytes 1540
  1212.1 33.2 %copy-start.21 = (f32[1,128]{1,0:T(1,128)S(1)}, f32[1,128]{1,0:T(1,128)}, u32[]{:S(2)}) copy-start(f32[1,128]{1,0:T(1,128)} %get-tuple-element.67) | copy-start | bytes 1540
  1212.1 33.2 %copy-start.37 = (s32[128]{0:T(128)S(1)}, s32[128]{0:T(128)}, u32[]{:S(2)}) copy-start(s32[128]{0:T(128)} %get-tuple-element.68) | copy-start | bytes 1540
  1217.8 38.0 %collective-permute-start.3 = (f32[3,195,384]{2,1,0:T(8,128)S(1)}, f32[3,195,384]{2,1,0:T(8,128)S(1)}, u32[]{:S(2)}, u32[]{:S(2)}) collective-permute-start(f32[3,195,384]{2,1,0:T(8,128)S(1)} %pad_maximum_fusion.3), channel_id=1, source_target_pairs={{2,0},{4,2},{6,4},{8,6},{10,8},{12,10},{14,12},{16,14},{18,16},{20... | collective-permute-start | bytes 2695688 | tf_op jit(solution)/shard_map/ppermute | solution.py:23
  1267.6 0.9 copy-start.39
